TPU v7x, 32 devices: a whole 2x2x4 slice. The times are simulated.
32 devices in a mesh: slab: 32 (over z, y, x, core).
Axes of the slice: x: 2, y: 2, z: 4, core: 2. Of those that a mesh axis runs over, the one named last changes fastest.
Arguments:
- offsets: float32 [2, 32, 16, 128], P(None, 'slab'), may hold values from 0 to 1
- velocity: float32 [2, 32, 16, 128], P(None, 'slab'), may hold values from -4 to 4
- affine: float32 [4, 32, 16, 128], P(None, 'slab'), may hold values from -1.5 to 1.5
- strain: float32 [4, 32, 16, 128], P(None, 'slab'), may hold values from -0.3 to 0.3
- tile_fill: int32 [32, 16], P('slab'), may hold values from 32 to 128
- force_field: float32 [2, 128, 1024], P(None, 'slab'), may hold values from -6 to 6
- cotangent: float32 [12, 32, 16, 128], P(None, 'slab'), may hold values from -6 to 6
Outputs:
- state_grad: float32 [12, 32, 16, 128], P(None, 'slab')
- force_grad: float32 [2, 128, 1024], P(None, 'slab')
All inputs are finite; a program needn't handle non-finite values.
Results may differ from a plain program's by a relative error of at most 0.0003.
Values sent between devices are 32-bit elements; how exact they have to be, the bound alone decides.
A program may use at most 64 MiB of HBM per device.

v0:
```python
import functools

import jax
import jax.numpy as jnp
from jax import lax
from jax.experimental import pallas as pl
from jax.experimental.pallas import tpu as pltpu
from jax.sharding import PartitionSpec as P

STEPS = 4
DT = 0.1
MASS_FLOOR = 0.25
STRESS = -0.4
F32 = jnp.float32


def row_terms(p0, r, slopes=False):
    d = float(r) - p0
    m = jnp.abs(d)
    t = jnp.maximum(1.5 - m, 0.0)
    inner = m < 0.5
    w = jnp.where(inner, 0.75 - m * m, 0.5 * t * t)
    wd = w * d
    if not slopes:
        return w, wd
    dw = jnp.where(inner, 2.0 * d, jnp.where(d > 0.0, t, -t))
    return w, wd, dw, dw * d - w


def col_terms(p1, width, slopes=False):
    base = jnp.floor(jnp.clip(p1, -8.0, width + 8.0) - 0.5)
    bi = base.astype(jnp.int32)
    f = p1 - base
    d = [-f, 1.0 - f, 2.0 - f]
    up, down = 1.5 - f, f - 0.5
    w = [0.5 * up * up, 0.75 - d[1] * d[1], 0.5 * down * down]
    dw = [-up, 2.0 * d[1], down]
    idx, ws, wds, dws, dwds = [], [], [], [], []
    for k in range(3):
        node = bi + k
        valid = (node >= 0) & (node < width)
        idx.append(node & (width - 1))
        wk = jnp.where(valid, w[k], 0.0)
        ws.append(wk)
        wds.append(jnp.where(valid, wk * d[k], 0.0))
        if slopes:
            dk = jnp.where(valid, dw[k], 0.0)
            dws.append(dk)
            dwds.append(jnp.where(valid, dk * d[k] - wk, 0.0))
    if slopes:
        return idx, ws, wds, dws, dwds
    return idx, ws, wds


def comb(c, g):
    return c[0] * g[0] + c[1] * g[1] + c[2] * g[2]


def take(x, idx):
    return [jnp.take_along_axis(x, i, axis=1, mode="promise_in_bounds") for i in idx]


def kernel(n, br, bc, off, vel, aff, strn, fill, force, cot, sg, fg,
           hist, adj, alive, asc, wsc, ohs, nodes, vgrid, inv, fs, fsum,
           fsend, frecv, bsend, brecv, send_sem, recv_sem):
    nq = off.shape[1] // 2
    ps = off.shape[2]
    width = 2 * bc
    nr = 2 * br
    half = br // 2
    shape = (nq, ps)
    me = lax.axis_index("slab")
    right, left = lax.rem(me + 1, n), lax.rem(me + n - 1, n)
    mesh_id = pl.DeviceIdType.MESH
    barrier = pltpu.get_barrier_semaphore()
    for nb in (left, right):
        pl.semaphore_signal(barrier, inc=1, device_id=(nb,), device_id_type=mesh_id)

    lane = lax.broadcasted_iota(jnp.int32, shape, 1)
    sub = lax.broadcasted_iota(jnp.int32, shape, 0)

    def odd_window(g):
        rolled = pltpu.roll(g, bc, 1)
        return jnp.where(lane < bc, rolled, pltpu.roll(rolled, nq - 1, 0))

    def window(g, h):
        return g if h == 0 else odd_window(g)

    for h in range(2):
        own = pl.ds(h, nq, stride=2)
        lim = jnp.zeros(shape, jnp.int32)
        for q in range(nq):
            lim = jnp.where(sub == q, fill[0, 2 * q + h], lim)
        live = jnp.where(lane < lim, 1.0, 0.0).astype(F32)
        alive[h] = live
        hist[0, 0, h] = br // 2 + br * off[0, own, :]
        hist[0, 1, h] = bc // 2 + bc * off[1, own, :]
        for a in range(2):
            hist[0, 2 + a, h] = vel[a, own, :]
        for a in range(4):
            hist[0, 4 + a, h] = aff[a, own, :]
            hist[0, 8 + a, h] = strn[a, own, :] + (1.0 if a in (0, 3) else 0.0)
        for a in range(12):
            adj[a, h] = cot[a, own, :] * live

    shift = bc // 2
    for a in range(2):
        for q in range(nq):
            fs[pl.ds(a * br * nq + q, br, stride=nq), :] = force[a, :, q * ps:(q + 1) * ps]
    for a in range(2):
        for r in range(br):
            at = pl.ds((a * br + r) * nq, nq)
            rolled = pltpu.roll(fs[at, :], shift, 1)
            fs[at, :] = DT * jnp.where(lane >= shift, rolled, pltpu.roll(rolled, 1, 0))
            fsum[at, :] = jnp.zeros(shape, F32)

    pl.semaphore_wait(barrier, 2)

    def fill_columns(h, r, comp, plain, slope, ws, wds):
        for k in range(3):
            val = ws[k] * plain if slope is None else ws[k] * plain + wds[k] * slope
            asc[pl.ds(((h * 9 + comp * 3 + k) * nr + r) * nq, nq), :] = val

    def scatter(comps, step, fresh):
        rows = comps * 3 * nr
        iota_j = lax.broadcasted_iota(jnp.int32, (width, ps), 0)
        for q in range(nq):
            for h in range(2):
                part = asc[pl.ds(h * 9 * nr * nq + q, rows, stride=nq), :]
                hi = part.astype(jnp.bfloat16)
                lo = (part - hi.astype(F32)).astype(jnp.bfloat16)
                if fresh:
                    row = nodes[h, pl.ds(q, 1), :]
                    hot = jnp.where(iota_j == row, 1.0, 0.0).astype(jnp.bfloat16)
                    ohs[step, 2 * q + h] = hot
                else:
                    hot = ohs[step, 2 * q + h]
                res = lax.dot_general(
                    jnp.concatenate([hi, lo], axis=1), jnp.concatenate([hot, hot], axis=1),
                    (((1,), (1,)), ((), ())), preferred_element_type=F32)
                for comp in range(comps):
                    at = comp * 3 * nr
                    out = (res[at:at + nr] + pltpu.roll(res[at + nr:at + 2 * nr], 1, 1)
                           + pltpu.roll(res[at + 2 * nr:at + 3 * nr], 2, 1))
                    wsc[pl.ds((h * 3 + comp) * nr * nq + q, nr, stride=nq), :] = out

    def grid_row(comp, r):
        even = wsc[pl.ds((comp * nr + r) * nq, nq), :]
        odd = pltpu.roll(wsc[pl.ds(((3 + comp) * nr + r) * nq, nq), :], bc, 1)
        return even + jnp.where(lane >= bc, odd, pltpu.roll(odd, 1, 0))

    def exchange(send, recv, slot, sem):
        copies = []
        for side, to in ((0, left), (1, right)):
            copies.append(pltpu.make_async_remote_copy(
                src_ref=send.at[slot, side], dst_ref=recv.at[slot, side],
                send_sem=send_sem.at[sem, side], recv_sem=recv_sem.at[sem, side],
                device_id=(to,), device_id_type=mesh_id))
        for c in copies:
            c.start()
        return copies

    def summed(send, recv, slot, comp, r):
        side, rr = r // br, r % br
        return send[slot, side, comp, rr] + recv[slot, 1 - side, comp, rr]

    def stress_terms(st, h):
        f00, f01, f10, f11 = (hist[st, 8 + a, h] for a in range(4))
        jac = f00 * f11 - f01 * f10
        return f00, f01, f10, f11, jac

    def moments(st, h):
        live = alive[h]
        f00, f01, f10, f11, jac = stress_terms(st, h)
        pressure = 2.0 * (jac - 1.0) * jac
        s = live * STRESS
        xx = s * (2.0 * (f00 * f00 + f01 * f01 - 1.0) + pressure)
        xy = s * (2.0 * (f00 * f10 + f01 * f11))
        yy = s * (2.0 * (f10 * f10 + f11 * f11 - 1.0) + pressure)
        c = [hist[st, 4 + a, h] * live for a in range(4)]
        x = [live * hist[st, 2, h], live * hist[st, 3, h]]
        return live, x, [xx + c[0], xy + c[1], xy + c[2], yy + c[3]]

    def forward(st, carry):
        for h in range(2):
            live, x, m = moments(st, h)
            p0 = hist[st, 0, h]
            idx, ws, wds = col_terms(hist[st, 1, h], width)
            nodes[h] = idx[0]
            mws = [live * w for w in ws]
            for r in range(nr):
                w, wd = row_terms(p0, r)
                fill_columns(h, r, 0, w, None, mws, None)
                for a in range(2):
                    fill_columns(h, r, 1 + a, w * x[a] + wd * m[2 * a], w * m[2 * a + 1], ws, wds)
        scatter(3, st, True)
        for comp in range(3):
            for r in range(nr):
                g = grid_row(comp, r)
                if comp > 0 and half <= r < half + br:
                    g = g + fs[pl.ds(((comp - 1) * br + r - half) * nq, nq), :]
                fsend[st, r // br, comp, r % br] = g
        copies = exchange(fsend, frecv, st, st)
        for c in copies:
            c.wait()
        for r in range(nr):
            iv = 1.0 / (summed(fsend, frecv, st, 0, r) + MASS_FLOOR)
            inv[st, r] = iv
            for a in range(2):
                vgrid[st, a, r] = summed(fsend, frecv, st, 1 + a, r) * iv
        for h in range(2):
            p0, p1 = hist[st, 0, h], hist[st, 1, h]
            idx, ws, wds = col_terms(p1, width)
            v = [0.0, 0.0]
            along_rows = [0.0, 0.0]
            along_cols = [0.0, 0.0]
            for r in range(nr):
                w, wd = row_terms(p0, r)
                for a in range(2):
                    g = take(window(vgrid[st, a, r], h), idx)
                    plain, slope = comb(ws, g), comb(wds, g)
                    v[a] = v[a] + w * plain
                    along_rows[a] = along_rows[a] + wd * plain
                    along_cols[a] = along_cols[a] + w * slope
            c00, c10 = 4.0 * along_rows[0], 4.0 * along_rows[1]
            c01, c11 = 4.0 * along_cols[0], 4.0 * along_cols[1]
            f00, f01, f10, f11 = (hist[st, 8 + a, h] for a in range(4))
            gxx, gxy, gyx, gyy = 1.0 + DT * c00, DT * c01, DT * c10, 1.0 + DT * c11
            new = [p0 + DT * v[0], p1 + DT * v[1], v[0], v[1], c00, c01, c10, c11,
                   gxx * f00 + gxy * f10, gxx * f01 + gxy * f11,
                   gyx * f00 + gyy * f10, gyx * f01 + gyy * f11]
            for a in range(12):
                hist[st + 1, a, h] = new[a]
        return carry

    lax.fori_loop(0, STEPS, forward, 0)

    def backward(i, carry):
        st = STEPS - 1 - i
        for h in range(2):
            ab = [adj[a, h] for a in range(12)]
            f00, f01, f10, f11 = (hist[st, 8 + a, h] for a in range(4))
            x = [ab[2] + DT * ab[0], ab[3] + DT * ab[1]]
            m = [4.0 * (ab[4] + DT * (ab[8] * f00 + ab[9] * f01)),
                 4.0 * (ab[5] + DT * (ab[8] * f10 + ab[9] * f11)),
                 4.0 * (ab[6] + DT * (ab[10] * f00 + ab[11] * f01)),
                 4.0 * (ab[7] + DT * (ab[10] * f10 + ab[11] * f11))]
            p0 = hist[st, 0, h]
            idx, ws, wds = col_terms(hist[st, 1, h], width)
            for r in range(nr):
                w, wd = row_terms(p0, r)
                for a in range(2):
                    fill_columns(h, r, a, w * x[a] + wd * m[2 * a], w * m[2 * a + 1], ws, wds)
            adj[2, h], adj[3, h] = x[0], x[1]
            for a in range(4):
                adj[4 + a, h] = m[a]
        scatter(2, st, False)
        for comp in range(2):
            for r in range(nr):
                bsend[st, r // br, comp, r % br] = grid_row(comp, r)
        copies = exchange(bsend, brecv, st, STEPS + st)
        for h in range(2):
            p0 = hist[st, 0, h]
            idx, ws, wds, dws, dwds = col_terms(hist[st, 1, h], width, True)
            x = [adj[2 + a, h] for a in range(2)]
            m = [adj[4 + a, h] for a in range(4)]
            dp0, dp1 = adj[0, h], adj[1, h]
            for r in range(nr):
                w, wd, dw, dwd = row_terms(p0, r, True)
                u = t = du = dt = 0.0
                for a in range(2):
                    g = take(window(vgrid[st, a, r], h), idx)
                    plain, slope = comb(ws, g), comb(wds, g)
                    dplain, dslope = comb(dws, g), comb(dwds, g)
                    u = u + x[a] * plain + m[2 * a + 1] * slope
                    t = t + m[2 * a] * plain
                    du = du + x[a] * dplain + m[2 * a + 1] * dslope
                    dt = dt + m[2 * a] * dplain
                dp0 = dp0 + dw * u + dwd * t
                dp1 = dp1 + w * du + wd * dt
            adj[0, h], adj[1, h] = dp0, dp1
            c00, c01, c10, c11 = (hist[st + 1, 4 + a, h] for a in range(4))
            b00, b01, b10, b11 = (adj[8 + a, h] for a in range(4))
            gxx, gxy, gyx, gyy = 1.0 + DT * c00, DT * c01, DT * c10, 1.0 + DT * c11
            adj[8, h] = gxx * b00 + gyx * b10
            adj[9, h] = gxx * b01 + gyx * b11
            adj[10, h] = gxy * b00 + gyy * b10
            adj[11, h] = gxy * b01 + gyy * b11
        for c in copies:
            c.wait()
        for r in range(nr):
            iv = inv[st, r]
            v0, v1 = summed(bsend, brecv, st, 0, r), summed(bsend, brecv, st, 1, r)
            m0, m1 = v0 * iv, v1 * iv
            gm = -(v0 * vgrid[st, 0, r] + v1 * vgrid[st, 1, r]) * iv
            for comp, g in enumerate((gm, m0, m1)):
                wsc[pl.ds((comp * nr + r) * nq, nq), :] = g
            if half <= r < half + br:
                for a, g in enumerate((m0, m1)):
                    at = pl.ds((a * br + r - half) * nq, nq)
                    fsum[at, :] = fsum[at, :] + DT * g
        for h in range(2):
            live, x, m = moments(st, h)
            p0 = hist[st, 0, h]
            idx, ws, wds, dws, dwds = col_terms(hist[st, 1, h], width, True)
            dp0, dp1 = adj[0, h], adj[1, h]
            dx = [0.0, 0.0]
            dm = [0.0, 0.0, 0.0, 0.0]
            for r in range(nr):
                w, wd, dw, dwd = row_terms(p0, r, True)
                g = take(window(wsc[pl.ds(r * nq, nq), :], h), idx)
                u, du = live * comb(ws, g), live * comb(dws, g)
                t = dt = 0.0
                for a in range(2):
                    g = take(window(wsc[pl.ds(((1 + a) * nr + r) * nq, nq), :], h), idx)
                    plain, slope = comb(ws, g), comb(wds, g)
                    dplain, dslope = comb(dws, g), comb(dwds, g)
                    dx[a] = dx[a] + w * plain
                    dm[2 * a] = dm[2 * a] + wd * plain
                    dm[2 * a + 1] = dm[2 * a + 1] + w * slope
                    u = u + x[a] * plain + m[2 * a + 1] * slope
                    t = t + m[2 * a] * plain
                    du = du + x[a] * dplain + m[2 * a + 1] * dslope
                    dt = dt + m[2 * a] * dplain
                dp0 = dp0 + dw * u + dwd * t
                dp1 = dp1 + w * du + wd * dt
            adj[0, h], adj[1, h] = dp0, dp1
            for a in range(2):
                adj[2 + a, h] = live * dx[a]
            dm = [live * y for y in dm]
            for a in range(4):
                adj[4 + a, h] = dm[a]
            f00, f01, f10, f11, jac = stress_terms(st, h)
            txx, tyy, txy = STRESS * dm[0], STRESS * dm[3], STRESS * (dm[1] + dm[2])
            dj = (txx + tyy) * (2.0 * (2.0 * jac - 1.0))
            adj[8, h] = adj[8, h] + 4.0 * f00 * txx + 2.0 * f10 * txy + dj * f11
            adj[9, h] = adj[9, h] + 4.0 * f01 * txx + 2.0 * f11 * txy - dj * f10
            adj[10, h] = adj[10, h] + 4.0 * f10 * tyy + 2.0 * f00 * txy - dj * f01
            adj[11, h] = adj[11, h] + 4.0 * f11 * tyy + 2.0 * f01 * txy + dj * f00
        return carry

    lax.fori_loop(0, STEPS, backward, 0)

    for h in range(2):
        for a in range(12):
            scale = float(br) if a == 0 else float(bc)
            val = adj[a, h]
            sg[a, pl.ds(h, nq, stride=2), :] = scale * val if a < 2 else val
    for a in range(2):
        for r in range(br):
            at = pl.ds((a * br + r) * nq, nq)
            rolled = pltpu.roll(fsum[at, :], ps - shift, 1)
            fsum[at, :] = jnp.where(lane < ps - shift, rolled, pltpu.roll(rolled, nq - 1, 0))
    for a in range(2):
        for q in range(nq):
            fg[a, :, q * ps:(q + 1) * ps] = fsum[pl.ds(a * br * nq + q, br, stride=nq), :]


def solution(mesh):
    n = mesh.shape["slab"]

    def per_device(offsets, velocity, affine, strain, tile_fill, force_field, cotangent):
        blocks, ps = offsets.shape[2:]
        bands = offsets.shape[1]
        br = force_field.shape[1] // bands
        bc = force_field.shape[2] // blocks
        assert bands == 1 and ps == 2 * bc and blocks % 2 == 0
        nq, nr = blocks // 2, 2 * br
        flat = lambda x: x.reshape(x.shape[0], blocks, ps)
        vmem = pl.BlockSpec(memory_space=pltpu.VMEM)
        smem = pl.BlockSpec(memory_space=pltpu.SMEM)
        tile = (nq, ps)
        sg, fg = pl.pallas_call(
            functools.partial(kernel, n, br, bc),
            out_shape=(jax.ShapeDtypeStruct((12, blocks, ps), F32),
                       jax.ShapeDtypeStruct(force_field.shape, F32)),
            in_specs=[vmem, vmem, vmem, vmem, smem, vmem, vmem],
            out_specs=(vmem, vmem),
            scratch_shapes=[
                pltpu.VMEM((STEPS + 1, 12, 2) + tile, F32),
                pltpu.VMEM((12, 2) + tile, F32),
                pltpu.VMEM((2,) + tile, F32),
                pltpu.VMEM((2 * 9 * nr * nq, ps), F32),
                pltpu.VMEM((2 * 3 * nr * nq, ps), F32),
                pltpu.VMEM((STEPS, blocks, 2 * bc, ps), jnp.bfloat16),
                pltpu.VMEM((2,) + tile, jnp.int32),
                pltpu.VMEM((STEPS, 2, nr) + tile, F32),
                pltpu.VMEM((STEPS, nr) + tile, F32),
                pltpu.VMEM((2 * br * nq, ps), F32),
                pltpu.VMEM((2 * br * nq, ps), F32),
                pltpu.VMEM((STEPS, 2, 3, br) + tile, F32),
                pltpu.VMEM((STEPS, 2, 3, br) + tile, F32),
                pltpu.VMEM((STEPS, 2, 2, br) + tile, F32),
                pltpu.VMEM((STEPS, 2, 2, br) + tile, F32),
                pltpu.SemaphoreType.DMA((2 * STEPS, 2)),
                pltpu.SemaphoreType.DMA((2 * STEPS, 2)),
            ],
            compiler_params=pltpu.CompilerParams(collective_id=0, has_side_effects=True),
        )(flat(offsets), flat(velocity), flat(affine), flat(strain), tile_fill, force_field, flat(cotangent))
        return sg.reshape(12, 1, blocks, ps), fg

    cut = P(None, "slab", None, None)
    return jax.shard_map(
        per_device,
        mesh=mesh,
        in_specs=(cut, cut, cut, cut, P("slab", None), P(None, "slab", None), cut),
        out_specs=(cut, P(None, "slab", None)),
        check_vma=False,
    )
```

profile of v0, /device:TPU:0, one launch (start us, length us, event | category | flops | bytes accessed | tf_op | source)
XLA Modules:
  0.0 59.0 jit_solution(17330922274562738681)
XLA Ops:
  0.6 56.2 %shard_map.86 = (f32[12,16,128]{2,1,0:T(8,128)}, f32[2,4,1024]{2,1,0:T(4,128)}) custom-call(f32[2,16,128]{2,1,0:T(8,128)} %bitcast.12, f32[2,16,128]{2,1,0:T(8,128)} %bitcast.13, f32[4,16,128]{2,1,0:T(8,128)} %bitcast.10, f32[4,16,128]{2,1,0:T(8,128)} %bitcast.11, s32[1,16]{1,0:T(1,128)} %fill.1, f32[2,4,1024]{2,1,0:T(4,128)} %force.1, f32[12,16,128]{2,1,0:T(8,128)} %bitcast.8), custom_call_target="tpu_custom_call" | custom-call | tf_op jit(solution)/shard_map/pallas_call | solution.py:373
  56.8 0.0 copy-start
  56.8 1.5 %copy.12 = f32[12,1,16,128]{3,2,1,0:T(8,128)} copy(f32[12,1,16,128]{3,2,1,0:T(8,128)} %bitcast.9) | data formatting | bytes 196608
  58.4 0.0 copy-done
  58.4 0.6 %copy.13 = f32[2,4,1024]{2,1,0:T(4,128)} copy(f32[2,4,1024]{2,1,0:T(4,128)S(1)} %copy-done) | data formatting | bytes 65536
Async XLA Ops:
  56.8 1.6 %copy-start = (f32[2,4,1024]{2,1,0:T(4,128)S(1)}, f32[2,4,1024]{2,1,0:T(4,128)}, u32[]{:S(2)}) copy-start(f32[2,4,1024]{2,1,0:T(4,128)} %get-tuple-element.11) | copy-start | bytes 98308
where the time goes:
time: 59.2 us; the launch traced here: 59 us
  Pallas kernels  56.2 us (95%)
  local copies, waits for them, and re-layouts  2.16 us (4%)
  between operations  0.65 us (1%)
    pallas_call x1, Pallas kernels, per_device(): pl.pallas_call(functools.partial(kernel, n, br, bc), out_shape=(jax.Shape...  56.2 us
    unnamed x4, local copies, waits for them, and re-layouts  2.16 us

commit v1 on v0

--- a/solution.py
+++ b/solution.py
@@ -15,7 +15,7 @@
 
 
 def row_terms(p0, r, slopes=False):
-    d = float(r) - p0
+    d = r - p0
     m = jnp.abs(d)
     t = jnp.maximum(1.5 - m, 0.0)
     inner = m < 0.5
@@ -61,7 +61,7 @@
 
 
 def kernel(n, br, bc, off, vel, aff, strn, fill, force, cot, sg, fg,
-           hist, adj, alive, asc, wsc, ohs, nodes, vgrid, inv, fs, fsum,
+           hist, adj, alive, asc, wsc, ohs, nodes, vgrid, inv, fs, fext, fsum,
            fsend, frecv, bsend, brecv, send_sem, recv_sem):
     nq = off.shape[1] // 2
     ps = off.shape[2]
@@ -71,6 +71,8 @@
     shape = (nq, ps)
     me = lax.axis_index("slab")
     right, left = lax.rem(me + 1, n), lax.rem(me + n - 1, n)
+    first = lax.rem(me // 2, 2)
+    near = 1 - lax.rem(me, 2)
     mesh_id = pl.DeviceIdType.MESH
     barrier = pltpu.get_barrier_semaphore()
     for nb in (left, right):
@@ -108,25 +110,32 @@
         for q in range(nq):
             fs[pl.ds(a * br * nq + q, br, stride=nq), :] = force[a, :, q * ps:(q + 1) * ps]
     for a in range(2):
+        for r in range(nr):
+            fsum[a, r] = jnp.zeros(shape, F32)
+            fext[a, r] = jnp.zeros(shape, F32)
         for r in range(br):
-            at = pl.ds((a * br + r) * nq, nq)
-            rolled = pltpu.roll(fs[at, :], shift, 1)
-            fs[at, :] = DT * jnp.where(lane >= shift, rolled, pltpu.roll(rolled, 1, 0))
-            fsum[at, :] = jnp.zeros(shape, F32)
+            rolled = pltpu.roll(fs[pl.ds((a * br + r) * nq, nq), :], shift, 1)
+            fext[a, r + half] = DT * jnp.where(lane >= shift, rolled, pltpu.roll(rolled, 1, 0))
+    asc[...] = jnp.zeros_like(asc)
 
     pl.semaphore_wait(barrier, 2)
 
-    def fill_columns(h, r, comp, plain, slope, ws, wds):
+    def padded(comps):
+        return -(-comps * br // 8) * 8
+
+    def fill_columns(phase, comps, h, rr, comp, plain, slope, ws, wds):
+        kb = padded(comps)
         for k in range(3):
             val = ws[k] * plain if slope is None else ws[k] * plain + wds[k] * slope
-            asc[pl.ds(((h * 9 + comp * 3 + k) * nr + r) * nq, nq), :] = val
-
-    def scatter(comps, step, fresh):
-        rows = comps * 3 * nr
+            at = ((phase * 2 + h) * 3 * padded(3) + k * kb + comp * br + rr) * nq
+            asc[pl.ds(at, nq), :] = val
+
+    def scatter(phase, comps, step, fresh):
+        kb = padded(comps)
         iota_j = lax.broadcasted_iota(jnp.int32, (width, ps), 0)
         for q in range(nq):
             for h in range(2):
-                part = asc[pl.ds(h * 9 * nr * nq + q, rows, stride=nq), :]
+                part = asc[pl.ds((phase * 2 + h) * 3 * padded(3) * nq + q, 3 * kb, stride=nq), :]
                 hi = part.astype(jnp.bfloat16)
                 lo = (part - hi.astype(F32)).astype(jnp.bfloat16)
                 if fresh:
@@ -138,30 +147,21 @@
                 res = lax.dot_general(
                     jnp.concatenate([hi, lo], axis=1), jnp.concatenate([hot, hot], axis=1),
                     (((1,), (1,)), ((), ())), preferred_element_type=F32)
-                for comp in range(comps):
-                    at = comp * 3 * nr
-                    out = (res[at:at + nr] + pltpu.roll(res[at + nr:at + 2 * nr], 1, 1)
-                           + pltpu.roll(res[at + 2 * nr:at + 3 * nr], 2, 1))
-                    wsc[pl.ds((h * 3 + comp) * nr * nq + q, nr, stride=nq), :] = out
-
-    def grid_row(comp, r):
-        even = wsc[pl.ds((comp * nr + r) * nq, nq), :]
-        odd = pltpu.roll(wsc[pl.ds(((3 + comp) * nr + r) * nq, nq), :], bc, 1)
+                out = res[:kb] + pltpu.roll(res[kb:2 * kb], 1, 1) + pltpu.roll(res[2 * kb:], 2, 1)
+                wsc[pl.ds((phase * 2 + h) * padded(3) * nq + q, kb, stride=nq), :] = out
+
+    def grid_row(phase, comp, rr):
+        even = wsc[pl.ds((phase * 2 * padded(3) + comp * br + rr) * nq, nq), :]
+        odd = pltpu.roll(wsc[pl.ds(((phase * 2 + 1) * padded(3) + comp * br + rr) * nq, nq), :], bc, 1)
         return even + jnp.where(lane >= bc, odd, pltpu.roll(odd, 1, 0))
 
-    def exchange(send, recv, slot, sem):
-        copies = []
-        for side, to in ((0, left), (1, right)):
-            copies.append(pltpu.make_async_remote_copy(
-                src_ref=send.at[slot, side], dst_ref=recv.at[slot, side],
-                send_sem=send_sem.at[sem, side], recv_sem=recv_sem.at[sem, side],
-                device_id=(to,), device_id_type=mesh_id))
-        for c in copies:
-            c.start()
-        return copies
-
-    def summed(send, recv, slot, comp, r):
-        side, rr = r // br, r % br
+    def copy_of(send, recv, slot, sem, side):
+        return pltpu.make_async_remote_copy(
+            src_ref=send.at[slot, side], dst_ref=recv.at[slot, side],
+            send_sem=send_sem.at[sem, side], recv_sem=recv_sem.at[sem, side],
+            device_id=(lax.rem(me + n - 1 + 2 * side, n),), device_id_type=mesh_id)
+
+    def summed(send, recv, slot, side, comp, rr):
         return send[slot, side, comp, rr] + recv[slot, 1 - side, comp, rr]
 
     def stress_terms(st, h):
@@ -182,46 +182,55 @@
         return live, x, [xx + c[0], xy + c[1], xy + c[2], yy + c[3]]
 
     def forward(st, carry):
-        for h in range(2):
-            live, x, m = moments(st, h)
-            p0 = hist[st, 0, h]
-            idx, ws, wds = col_terms(hist[st, 1, h], width)
-            nodes[h] = idx[0]
-            mws = [live * w for w in ws]
-            for r in range(nr):
-                w, wd = row_terms(p0, r)
-                fill_columns(h, r, 0, w, None, mws, None)
+        cols = []
+        for h in range(2):
+            cols.append(col_terms(hist[st, 1, h], width))
+            nodes[h] = cols[h][0][0]
+        for phase in range(2):
+            side = first if phase == 0 else 1 - first
+            for h in range(2):
+                live, x, m = moments(st, h)
+                p0 = hist[st, 0, h]
+                idx, ws, wds = cols[h]
+                mws = [live * w for w in ws]
+                for rr in range(br):
+                    w, wd = row_terms(p0, (side * br + rr).astype(F32))
+                    fill_columns(phase, 3, h, rr, 0, w, None, mws, None)
+                    for a in range(2):
+                        fill_columns(phase, 3, h, rr, 1 + a, w * x[a] + wd * m[2 * a], w * m[2 * a + 1], ws, wds)
+            scatter(phase, 3, st, phase == 0)
+            for comp in range(3):
+                for rr in range(br):
+                    g = grid_row(phase, comp, rr)
+                    if comp > 0:
+                        g = g + fext[comp - 1, side * br + rr]
+                    fsend[st, side, comp, rr] = g
+            copy_of(fsend, frecv, st, st, side).start()
+        acc = [[0.0] * 6 for h in range(2)]
+        for part in range(2):
+            side = near if part == 0 else 1 - near
+            copy_of(fsend, frecv, st, st, 1 - side).wait_recv()
+            for rr in range(br):
+                r = side * br + rr
+                iv = 1.0 / (summed(fsend, frecv, st, side, 0, rr) + MASS_FLOOR)
+                inv[st, r] = iv
+                vg = [summed(fsend, frecv, st, side, 1 + a, rr) * iv for a in range(2)]
                 for a in range(2):
-                    fill_columns(h, r, 1 + a, w * x[a] + wd * m[2 * a], w * m[2 * a + 1], ws, wds)
-        scatter(3, st, True)
-        for comp in range(3):
-            for r in range(nr):
-                g = grid_row(comp, r)
-                if comp > 0 and half <= r < half + br:
-                    g = g + fs[pl.ds(((comp - 1) * br + r - half) * nq, nq), :]
-                fsend[st, r // br, comp, r % br] = g
-        copies = exchange(fsend, frecv, st, st)
-        for c in copies:
-            c.wait()
-        for r in range(nr):
-            iv = 1.0 / (summed(fsend, frecv, st, 0, r) + MASS_FLOOR)
-            inv[st, r] = iv
-            for a in range(2):
-                vgrid[st, a, r] = summed(fsend, frecv, st, 1 + a, r) * iv
+                    vgrid[st, a, r] = vg[a]
+                for h in range(2):
+                    idx, ws, wds = cols[h]
+                    w, wd = row_terms(hist[st, 0, h], r.astype(F32))
+                    for a in range(2):
+                        g = take(window(vg[a], h), idx)
+                        plain, slope = comb(ws, g), comb(wds, g)
+                        acc[h][a] = acc[h][a] + w * plain
+                        acc[h][2 + a] = acc[h][2 + a] + wd * plain
+                        acc[h][4 + a] = acc[h][4 + a] + w * slope
+        for side in range(2):
+            copy_of(fsend, frecv, st, st, side).wait_send()
         for h in range(2):
             p0, p1 = hist[st, 0, h], hist[st, 1, h]
-            idx, ws, wds = col_terms(p1, width)
-            v = [0.0, 0.0]
-            along_rows = [0.0, 0.0]
-            along_cols = [0.0, 0.0]
-            for r in range(nr):
-                w, wd = row_terms(p0, r)
-                for a in range(2):
-                    g = take(window(vgrid[st, a, r], h), idx)
-                    plain, slope = comb(ws, g), comb(wds, g)
-                    v[a] = v[a] + w * plain
-                    along_rows[a] = along_rows[a] + wd * plain
-                    along_cols[a] = along_cols[a] + w * slope
+            v, along_rows, along_cols = acc[h][0:2], acc[h][2:4], acc[h][4:6]
             c00, c10 = 4.0 * along_rows[0], 4.0 * along_rows[1]
             c01, c11 = 4.0 * along_cols[0], 4.0 * along_cols[1]
             f00, f01, f10, f11 = (hist[st, 8 + a, h] for a in range(4))
@@ -245,20 +254,25 @@
                  4.0 * (ab[5] + DT * (ab[8] * f10 + ab[9] * f11)),
                  4.0 * (ab[6] + DT * (ab[10] * f00 + ab[11] * f01)),
                  4.0 * (ab[7] + DT * (ab[10] * f10 + ab[11] * f11))]
-            p0 = hist[st, 0, h]
-            idx, ws, wds = col_terms(hist[st, 1, h], width)
-            for r in range(nr):
-                w, wd = row_terms(p0, r)
-                for a in range(2):
-                    fill_columns(h, r, a, w * x[a] + wd * m[2 * a], w * m[2 * a + 1], ws, wds)
             adj[2, h], adj[3, h] = x[0], x[1]
             for a in range(4):
                 adj[4 + a, h] = m[a]
-        scatter(2, st, False)
-        for comp in range(2):
-            for r in range(nr):
-                bsend[st, r // br, comp, r % br] = grid_row(comp, r)
-        copies = exchange(bsend, brecv, st, STEPS + st)
+        for phase in range(2):
+            side = first if phase == 0 else 1 - first
+            for h in range(2):
+                x = [adj[2 + a, h] for a in range(2)]
+                m = [adj[4 + a, h] for a in range(4)]
+                p0 = hist[st, 0, h]
+                idx, ws, wds = col_terms(hist[st, 1, h], width)
+                for rr in range(br):
+                    w, wd = row_terms(p0, (side * br + rr).astype(F32))
+                    for a in range(2):
+                        fill_columns(phase, 2, h, rr, a, w * x[a] + wd * m[2 * a], w * m[2 * a + 1], ws, wds)
+            scatter(phase, 2, st, False)
+            for comp in range(2):
+                for rr in range(br):
+                    bsend[st, side, comp, rr] = grid_row(phase, comp, rr)
+            copy_of(bsend, brecv, st, STEPS + st, side).start()
         for h in range(2):
             p0 = hist[st, 0, h]
             idx, ws, wds, dws, dwds = col_terms(hist[st, 1, h], width, True)
@@ -266,7 +280,7 @@
             m = [adj[4 + a, h] for a in range(4)]
             dp0, dp1 = adj[0, h], adj[1, h]
             for r in range(nr):
-                w, wd, dw, dwd = row_terms(p0, r, True)
+                w, wd, dw, dwd = row_terms(p0, float(r), True)
                 u = t = du = dt = 0.0
                 for a in range(2):
                     g = take(window(vgrid[st, a, r], h), idx)
@@ -286,44 +300,45 @@
             adj[9, h] = gxx * b01 + gyx * b11
             adj[10, h] = gxy * b00 + gyy * b10
             adj[11, h] = gxy * b01 + gyy * b11
-        for c in copies:
-            c.wait()
-        for r in range(nr):
-            iv = inv[st, r]
-            v0, v1 = summed(bsend, brecv, st, 0, r), summed(bsend, brecv, st, 1, r)
-            m0, m1 = v0 * iv, v1 * iv
-            gm = -(v0 * vgrid[st, 0, r] + v1 * vgrid[st, 1, r]) * iv
-            for comp, g in enumerate((gm, m0, m1)):
-                wsc[pl.ds((comp * nr + r) * nq, nq), :] = g
-            if half <= r < half + br:
-                for a, g in enumerate((m0, m1)):
-                    at = pl.ds((a * br + r - half) * nq, nq)
-                    fsum[at, :] = fsum[at, :] + DT * g
-        for h in range(2):
-            live, x, m = moments(st, h)
-            p0 = hist[st, 0, h]
-            idx, ws, wds, dws, dwds = col_terms(hist[st, 1, h], width, True)
-            dp0, dp1 = adj[0, h], adj[1, h]
-            dx = [0.0, 0.0]
-            dm = [0.0, 0.0, 0.0, 0.0]
-            for r in range(nr):
-                w, wd, dw, dwd = row_terms(p0, r, True)
-                g = take(window(wsc[pl.ds(r * nq, nq), :], h), idx)
-                u, du = live * comb(ws, g), live * comb(dws, g)
-                t = dt = 0.0
+        parts = []
+        for h in range(2):
+            parts.append([moments(st, h), col_terms(hist[st, 1, h], width, True), [0.0] * 6,
+                          [adj[0, h], adj[1, h]]])
+        for part in range(2):
+            side = near if part == 0 else 1 - near
+            copy_of(bsend, brecv, st, STEPS + st, 1 - side).wait_recv()
+            for rr in range(br):
+                r = side * br + rr
+                iv = inv[st, r]
+                v0, v1 = (summed(bsend, brecv, st, side, a, rr) for a in range(2))
+                gs = [v0 * iv, v1 * iv]
+                gm = -(v0 * vgrid[st, 0, r] + v1 * vgrid[st, 1, r]) * iv
                 for a in range(2):
-                    g = take(window(wsc[pl.ds(((1 + a) * nr + r) * nq, nq), :], h), idx)
-                    plain, slope = comb(ws, g), comb(wds, g)
-                    dplain, dslope = comb(dws, g), comb(dwds, g)
-                    dx[a] = dx[a] + w * plain
-                    dm[2 * a] = dm[2 * a] + wd * plain
-                    dm[2 * a + 1] = dm[2 * a + 1] + w * slope
-                    u = u + x[a] * plain + m[2 * a + 1] * slope
-                    t = t + m[2 * a] * plain
-                    du = du + x[a] * dplain + m[2 * a + 1] * dslope
-                    dt = dt + m[2 * a] * dplain
-                dp0 = dp0 + dw * u + dwd * t
-                dp1 = dp1 + w * du + wd * dt
+                    fsum[a, r] = fsum[a, r] + DT * gs[a]
+                for h in range(2):
+                    (live, x, m), (idx, ws, wds, dws, dwds), acc, dp = parts[h]
+                    w, wd, dw, dwd = row_terms(hist[st, 0, h], r.astype(F32), True)
+                    g = take(window(gm, h), idx)
+                    u, du = live * comb(ws, g), live * comb(dws, g)
+                    t = dt = 0.0
+                    for a in range(2):
+                        g = take(window(gs[a], h), idx)
+                        plain, slope = comb(ws, g), comb(wds, g)
+                        dplain, dslope = comb(dws, g), comb(dwds, g)
+                        acc[a] = acc[a] + w * plain
+                        acc[2 + 2 * a] = acc[2 + 2 * a] + wd * plain
+                        acc[3 + 2 * a] = acc[3 + 2 * a] + w * slope
+                        u = u + x[a] * plain + m[2 * a + 1] * slope
+                        t = t + m[2 * a] * plain
+                        du = du + x[a] * dplain + m[2 * a + 1] * dslope
+                        dt = dt + m[2 * a] * dplain
+                    dp[0] = dp[0] + dw * u + dwd * t
+                    dp[1] = dp[1] + w * du + wd * dt
+        for side in range(2):
+            copy_of(bsend, brecv, st, STEPS + st, side).wait_send()
+        for h in range(2):
+            (live, x, m), _, acc, (dp0, dp1) = parts[h]
+            dx, dm = acc[:2], acc[2:]
             adj[0, h], adj[1, h] = dp0, dp1
             for a in range(2):
                 adj[2 + a, h] = live * dx[a]
@@ -348,12 +363,12 @@
             sg[a, pl.ds(h, nq, stride=2), :] = scale * val if a < 2 else val
     for a in range(2):
         for r in range(br):
-            at = pl.ds((a * br + r) * nq, nq)
-            rolled = pltpu.roll(fsum[at, :], ps - shift, 1)
-            fsum[at, :] = jnp.where(lane < ps - shift, rolled, pltpu.roll(rolled, nq - 1, 0))
+            rolled = pltpu.roll(fsum[a, half + r], ps - shift, 1)
+            fs[pl.ds((a * br + r) * nq, nq), :] = jnp.where(
+                lane < ps - shift, rolled, pltpu.roll(rolled, nq - 1, 0))
     for a in range(2):
         for q in range(nq):
-            fg[a, :, q * ps:(q + 1) * ps] = fsum[pl.ds(a * br * nq + q, br, stride=nq), :]
+            fg[a, :, q * ps:(q + 1) * ps] = fs[pl.ds(a * br * nq + q, br, stride=nq), :]
 
 
 def solution(mesh):
@@ -366,6 +381,7 @@
         bc = force_field.shape[2] // blocks
         assert bands == 1 and ps == 2 * bc and blocks % 2 == 0
         nq, nr = blocks // 2, 2 * br
+        pad = -(-3 * br // 8) * 8
         flat = lambda x: x.reshape(x.shape[0], blocks, ps)
         vmem = pl.BlockSpec(memory_space=pltpu.VMEM)
         smem = pl.BlockSpec(memory_space=pltpu.SMEM)
@@ -380,14 +396,15 @@
                 pltpu.VMEM((STEPS + 1, 12, 2) + tile, F32),
                 pltpu.VMEM((12, 2) + tile, F32),
                 pltpu.VMEM((2,) + tile, F32),
-                pltpu.VMEM((2 * 9 * nr * nq, ps), F32),
-                pltpu.VMEM((2 * 3 * nr * nq, ps), F32),
+                pltpu.VMEM((4 * 3 * pad * nq, ps), F32),
+                pltpu.VMEM((4 * pad * nq, ps), F32),
                 pltpu.VMEM((STEPS, blocks, 2 * bc, ps), jnp.bfloat16),
                 pltpu.VMEM((2,) + tile, jnp.int32),
                 pltpu.VMEM((STEPS, 2, nr) + tile, F32),
                 pltpu.VMEM((STEPS, nr) + tile, F32),
                 pltpu.VMEM((2 * br * nq, ps), F32),
-                pltpu.VMEM((2 * br * nq, ps), F32),
+                pltpu.VMEM((2, nr) + tile, F32),
+                pltpu.VMEM((2, nr) + tile, F32),
                 pltpu.VMEM((STEPS, 2, 3, br) + tile, F32),
                 pltpu.VMEM((STEPS, 2, 3, br) + tile, F32),
                 pltpu.VMEM((STEPS, 2, 2, br) + tile, F32),

time: 59.2 us -> 53.7 us (0.907)
  Pallas kernels: 56.2 us -> 50.7 us
    pallas_call x1, Pallas kernels: 56.2 us -> 50.7 us  [per_device(): pl.pallas_call(functools.partial(kernel, n, br, bc), out_shape=(jax.Shape...]
where the time goes in v1:
time: 53.7 us; the launch traced here: 53.6 us
  Pallas kernels  50.7 us (94%)
  local copies, waits for them, and re-layouts  2.16 us (4%)
  between operations  0.65 us (1%)
    pallas_call x1, Pallas kernels, per_device(): pl.pallas_call(functools.partial(kernel, n, br, bc), out_shape=(jax.Shape...  50.7 us
    unnamed x4, local copies, waits for them, and re-layouts  2.16 us

profile of v1, /device:TPU:0, one launch (start us, length us, event | category | flops | bytes accessed | tf_op | source)
XLA Modules:
  0.0 53.6 jit_solution(9514053288080719324)
XLA Ops:
  0.6 50.7 %shard_map.86 = (f32[12,16,128]{2,1,0:T(8,128)}, f32[2,4,1024]{2,1,0:T(4,128)}) custom-call(f32[2,16,128]{2,1,0:T(8,128)} %bitcast.12, f32[2,16,128]{2,1,0:T(8,128)} %bitcast.13, f32[4,16,128]{2,1,0:T(8,128)} %bitcast.10, f32[4,16,128]{2,1,0:T(8,128)} %bitcast.11, s32[1,16]{1,0:T(1,128)} %fill.1, f32[2,4,1024]{2,1,0:T(4,128)} %force.1, f32[12,16,128]{2,1,0:T(8,128)} %bitcast.8), custom_call_target="tpu_custom_call" | custom-call | tf_op jit(solution)/shard_map/pallas_call | solution.py:389
  51.4 0.0 copy-start
  51.4 1.5 %copy.12 = f32[12,1,16,128]{3,2,1,0:T(8,128)} copy(f32[12,1,16,128]{3,2,1,0:T(8,128)} %bitcast.9) | data formatting | bytes 196608
  52.9 0.0 copy-done
  52.9 0.6 %copy.13 = f32[2,4,1024]{2,1,0:T(4,128)} copy(f32[2,4,1024]{2,1,0:T(4,128)S(1)} %copy-done) | data formatting | bytes 65536
Async XLA Ops:
  51.4 1.6 %copy-start = (f32[2,4,1024]{2,1,0:T(4,128)S(1)}, f32[2,4,1024]{2,1,0:T(4,128)}, u32[]{:S(2)}) copy-start(f32[2,4,1024]{2,1,0:T(4,128)} %get-tuple-element.11) | copy-start | bytes 98308
